TPU v7x, 32 devices: a whole 2x2x4 slice. The times are simulated.
32 devices in a mesh: slab: 8 (over z, y), patch: 4 (over x, core).
Axes of the slice: x: 2, y: 2, z: 4, core: 2. Of those that a mesh axis runs over, the one named last changes fastest.
Arguments:
- fluid_state: float32 [16, 256, 256], P('slab', 'patch'), may hold values from -6 to 6
- fluid_rhs: float32 [16, 256, 256], P('slab', 'patch'), may hold values from -24 to 24
- element_scale: float32 [16, 256], P('slab', 'patch'), may hold values from 1 to 4
- element_matrix: bfloat16 [256, 256], replicated
- couple_x: bfloat16 [256, 256], replicated, may hold values from -0.09375 to 0.09375
- couple_y: bfloat16 [256, 256], replicated, may hold values from -0.09375 to 0.09375
- block_inverse: bfloat16 [256, 256], replicated
- traction_map: bfloat16 [3, 256], replicated, may hold values from -0.375 to 0.375
- slot_elem: int32 [8, 4, 1024], P('slab', 'patch'), may hold values from 0 to 127
- slot_point: int32 [8, 4, 1024], P('slab', 'patch'), may hold values from 0 to 8191
- slot_count: int32 [8, 4, 4], P('slab', 'patch'), may hold values from 0 to 256, as said below
- displacement: float32 [3, 256, 128], P(None, 'patch'), may hold values from -6 to 6
- stiffness: float32 [256, 128], P('patch'), may hold values from 0.03 to 0.3
Outputs:
- fluid_out: float32 [16, 256, 256], P('slab', 'patch')
- displacement_new: float32 [3, 256, 128], P(None, 'patch')
- wall_motion: float32 [3, 8, 4, 1024], P(None, 'slab', 'patch')
Inputs may be any that keep to these rules, and one draw needn't show every extreme that they name: For every block and owner only the first slot_count slots of that owner's 256 slots are live; the count 256 is reached for some block and owner in every draw.
All inputs are finite; a program needn't handle non-finite values.
Results may differ from a plain program's by a relative error of at most 0.0049.
Values may be sent and summed in bfloat16 or wider, within the bound.
A program may use at most 128 MiB of HBM per device.

v0:
```python
import jax
import jax.numpy as jnp
from jax import lax
from jax.sharding import PartitionSpec as P

SWEEPS = 3


def with_halo(cells, sides, width):
    for axis, dim in sides:
        count = lax.axis_size(axis)
        ends = count - 1
        head = lax.slice_in_dim(cells, 0, width, axis=dim)
        tail = lax.slice_in_dim(cells, cells.shape[dim] - width, cells.shape[dim], axis=dim)
        cells = jnp.concatenate(
            [
                lax.ppermute(tail, axis, [(i, (i + 1) % count) for i in range(ends)]),
                cells,
                lax.ppermute(head, axis, [((i + 1) % count, i) for i in range(ends)]),
            ],
            axis=dim,
        )
    return cells


def element_apply(rounded, scale, element_matrix, couple_x, couple_y):
    padded = with_halo(rounded, (("slab", 0), ("patch", 1)), 1)
    along_x = (padded[:-2, 1:-1].astype(jnp.float32) + padded[2:, 1:-1].astype(jnp.float32)).astype(
        jnp.bfloat16
    )
    along_y = (padded[1:-1, :-2].astype(jnp.float32) + padded[1:-1, 2:].astype(jnp.float32)).astype(
        jnp.bfloat16
    )
    width = rounded.shape[2]
    own = jnp.dot(rounded.reshape(-1, width), element_matrix, preferred_element_type=jnp.float32)
    side_x = jnp.dot(along_x.reshape(-1, width), couple_x, preferred_element_type=jnp.float32)
    side_y = jnp.dot(along_y.reshape(-1, width), couple_y, preferred_element_type=jnp.float32)
    return (
        scale[:, :, None] * own.reshape(rounded.shape)
        - side_x.reshape(rounded.shape)
        - side_y.reshape(rounded.shape)
    )


def laplace_net(field):
    edged = with_halo(field.astype(jnp.bfloat16), (("patch", 1),), 1).astype(field.dtype)
    edged = jnp.pad(edged, ((0, 0), (0, 0), (1, 1)))
    return 4.0 * field - (
        edged[:, 2:, 1:-1] + edged[:, :-2, 1:-1] + edged[:, 1:-1, 2:] + edged[:, 1:-1, :-2]
    )


def shards(
    fluid_state,
    fluid_rhs,
    element_scale,
    element_matrix,
    couple_x,
    couple_y,
    block_inverse,
    traction_map,
    slot_elem,
    slot_point,
    slot_count,
    displacement,
    stiffness,
):
    width = fluid_state.shape[2]
    state = fluid_state
    for sweep in range(SWEEPS):
        rounded = state.astype(jnp.bfloat16)
        applied = element_apply(rounded, element_scale, element_matrix, couple_x, couple_y)
        residue = (fluid_rhs - applied).astype(jnp.bfloat16)
        update = jnp.dot(
            residue.reshape(-1, width), block_inverse, preferred_element_type=jnp.float32
        ).reshape(state.shape)
        state = state + update / element_scale[:, :, None]
    final = state.astype(jnp.bfloat16)
    owners = lax.axis_size("patch")
    capacity = slot_elem.shape[2] // owners
    net_rows = displacement.shape[1]
    net_cols = displacement.shape[2]
    cells = net_rows * net_cols
    rows = jnp.take(final.reshape(-1, width), slot_elem.reshape(-1), axis=0).reshape(
        owners, capacity, width
    )
    pull = jnp.einsum("cd,kqd->kcq", traction_map, rows, preferred_element_type=jnp.float32)
    limits = slot_count.reshape(owners)
    live = (lax.broadcasted_iota(jnp.int32, (owners, capacity), 1) < limits[:, None]).astype(
        jnp.float32
    )
    pull = pull * live[:, None, :]
    points = slot_point.reshape(owners, capacity)
    owner_ids = lax.broadcasted_iota(jnp.int32, (owners, capacity), 0)
    got_pull, got_points = (
        lax.all_to_all(pull, "patch", split_axis=0, concat_axis=0, tiled=True),
        lax.all_to_all(points, "patch", split_axis=0, concat_axis=0, tiled=True),
    )
    local = jnp.zeros((3, cells), jnp.float32)
    local = local.at[:, got_points.reshape(-1)].add(got_pull.transpose(1, 0, 2).reshape(3, -1))
    loads = lax.psum(local, "slab")
    loads = loads.reshape(3, net_rows, net_cols)
    bend = laplace_net(displacement)
    stiff_term = stiffness[None] * (laplace_net(bend) + 4.0 * bend)
    displacement_new = displacement + (loads - stiff_term) / (36.0 * stiffness[None])
    flat_net = displacement_new.reshape(3, -1)
    whole = lax.all_gather(flat_net, "patch", axis=1, tiled=True)
    picked = whole[:, (owner_ids * cells + points).reshape(-1)]
    wall_motion = (picked * live.reshape(1, -1)).reshape(3, 1, 1, owners * capacity)
    return (state, displacement_new, wall_motion)


def solution(mesh):
    return jax.shard_map(
        shards,
        mesh=mesh,
        in_specs=(
            P("slab", "patch", None),
            P("slab", "patch", None),
            P("slab", "patch"),
            P(),
            P(),
            P(),
            P(),
            P(),
            P("slab", "patch", None),
            P("slab", "patch", None),
            P("slab", "patch", None),
            P(None, "patch", None),
            P("patch", None),
        ),
        out_specs=(
            P("slab", "patch", None),
            P(None, "patch", None),
            P(None, "slab", "patch", None),
        ),
        check_vma=False,
    )
```

profile of v0, /device:TPU:0, one launch (start us, length us, event | category | flops | bytes accessed | tf_op | source)
XLA Modules:
  0.0 299.1 jit_solution(18253544204650045127)
XLA Ops:
  7.2 0.0 copy-start
  7.2 0.0 copy-start.6
  7.2 0.0 copy-start.1
  7.2 0.0 copy-start.2
  7.2 0.0 copy-start.7
  7.2 0.0 copy-start.8
  7.2 1.0 convert_element_type.106
  8.3 1.3 collective-permute-start.1
  9.6 5.5 %collective-permute-start = (bf16[1,64,256]{2,1,0:T(8,128)(2,1)S(1)}, bf16[1,64,256]{2,1,0:T(8,128)(2,1)S(1)}, u32[]{:S(2)}, u32[]{:S(2)}) collective-permute-start(bf16[1,64,256]{2,1,0:T(8,128)(2,1)S(1)} %get-tuple-element.24), channel_id=1, source_target_pairs={{0,4},{4,8},{8,12},{12,16},{16,20},{20,24},{24,28},{1,5},{5,9},{9,... | collective-permute-start | bytes 98312 | tf_op jit(solution)/shard_map/ppermute | solution.py:17
  15.1 3.3 %all-to-all-start = ((s32[4,1,256]{2,1,0:T(1,128)}), s32[4,1,256]{2,1,0:T(1,128)S(1)}, u32[]{:S(2)}, u32[]{:S(2)}) async-start(s32[4,1,256]{2,1,0:T(1,128)} %bitcast.90), calls=%async_computation | async-start | bytes 8192 | tf_op jit(solution)/shard_map/all_to_all | solution.py:97
  18.4 0.9 convert_element_type.132
  19.3 1.3 collective-permute-start.13
  20.6 3.0 %collective-permute-start.12 = (bf16[3,1,128]{2,1,0:T(2,128)(2,1)S(1)}, bf16[3,1,128]{2,1,0:T(2,128)(2,1)S(1)}, u32[]{:S(2)}, u32[]{:S(2)}) collective-permute-start(bf16[3,1,128]{2,1,0:T(2,128)(2,1)S(1)} %get-tuple-element.28), channel_id=1, source_target_pairs={{0,1},{1,2},{2,3},{4,5},{5,6},{6,7},{8,9},{9,10},{10,11},{12,13},{... | collective-permute-start | bytes 2312 | tf_op jit(solution)/shard_map/ppermute | solution.py:17
  23.7 0.7 compare_select_fusion.1
  24.4 0.5 broadcast.126
  24.9 1.3 reduce.3
  26.2 0.8 broadcast_multiply_fusion
  27.0 0.1 broadcast_bitcast_fusion
  27.1 0.7 compare_select_fusion
  27.8 1.1 convolution_multiply_fusion.2
  28.8 0.7 fusion.59
  29.6 1.0 fusion.70
  30.7 1.3 collective-permute-start.15
  32.0 4.3 %collective-permute-start.14 = (bf16[3,1,128]{2,1,0:T(2,128)(2,1)S(1)}, bf16[3,1,128]{2,1,0:T(2,128)(2,1)S(1)}, u32[]{:S(2)}, u32[]{:S(2)}) collective-permute-start(bf16[3,1,128]{2,1,0:T(2,128)(2,1)S(1)} %get-tuple-element.26), channel_id=1, source_target_pairs={{0,1},{1,2},{2,3},{4,5},{5,6},{6,7},{8,9},{9,10},{10,11},{12,13},{... | collective-permute-start | bytes 2312 | tf_op jit(solution)/shard_map/ppermute | solution.py:17
  36.3 1.3 collective-permute-start.3
  37.6 4.3 %collective-permute-start.2 = (bf16[4,1,256]{2,1,0:T(2,128)(2,1)S(1)}, bf16[4,1,256]{2,1,0:T(2,128)(2,1)S(1)}, u32[]{:S(2)}, u32[]{:S(2)}) collective-permute-start(bf16[4,1,256]{2,1,0:T(2,128)(2,1)S(1)} %get-tuple-element.18), channel_id=1, source_target_pairs={{0,1},{1,2},{2,3},{4,5},{5,6},{6,7},{8,9},{9,10},{10,11},{12,13},{... | collective-permute-start | bytes 6152 | tf_op jit(solution)/shard_map/ppermute | solution.py:17
  41.9 1.1 convolution_subtract_fusion.5
  43.0 1.3 fusion.77
  44.3 1.3 collective-permute-start.5
  45.6 5.4 %collective-permute-start.4 = (bf16[1,64,256]{2,1,0:T(8,128)(2,1)S(1)}, bf16[1,64,256]{2,1,0:T(8,128)(2,1)S(1)}, u32[]{:S(2)}, u32[]{:S(2)}) collective-permute-start(bf16[1,64,256]{2,1,0:T(8,128)(2,1)S(1)} %get-tuple-element.22), channel_id=1, source_target_pairs={{0,4},{4,8},{8,12},{12,16},{16,20},{20,24},{24,28},{1,5},{5,9},{9,... | collective-permute-start | bytes 98312 | tf_op jit(solution)/shard_map/ppermute | solution.py:17
  51.1 1.1 convolution_multiply_fusion.1
  52.1 0.5 collective-permute-done.4
  52.6 1.3 collective-permute-start.7
  53.9 3.5 %collective-permute-start.6 = (bf16[4,1,256]{2,1,0:T(2,128)(2,1)S(1)}, bf16[4,1,256]{2,1,0:T(2,128)(2,1)S(1)}, u32[]{:S(2)}, u32[]{:S(2)}) collective-permute-start(bf16[4,1,256]{2,1,0:T(2,128)(2,1)S(1)} %get-tuple-element.16), channel_id=1, source_target_pairs={{0,1},{1,2},{2,3},{4,5},{5,6},{6,7},{8,9},{9,10},{10,11},{12,13},{... | collective-permute-start | bytes 6152 | tf_op jit(solution)/shard_map/ppermute | solution.py:17
  57.5 0.2 convolution_subtract_fusion.3
  57.6 0.0 copy-start.9
  57.7 0.6 collective-permute-done.6
  58.3 0.3 fusion.80
  58.6 1.3 collective-permute-start.9
  59.9 5.2 %collective-permute-start.8 = (bf16[1,64,256]{2,1,0:T(8,128)(2,1)S(1)}, bf16[1,64,256]{2,1,0:T(8,128)(2,1)S(1)}, u32[]{:S(2)}, u32[]{:S(2)}) collective-permute-start(bf16[1,64,256]{2,1,0:T(8,128)(2,1)S(1)} %get-tuple-element.20), channel_id=1, source_target_pairs={{0,4},{4,8},{8,12},{12,16},{16,20},{20,24},{24,28},{1,5},{5,9},{9,... | collective-permute-start | bytes 98312 | tf_op jit(solution)/shard_map/ppermute | solution.py:17
  65.1 0.2 convolution_multiply_fusion
  65.3 1.4 collective-permute-done.8
  66.7 1.3 collective-permute-start.11
  68.0 4.5 %collective-permute-start.10 = (bf16[4,1,256]{2,1,0:T(2,128)(2,1)S(1)}, bf16[4,1,256]{2,1,0:T(2,128)(2,1)S(1)}, u32[]{:S(2)}, u32[]{:S(2)}) collective-permute-start(bf16[4,1,256]{2,1,0:T(2,128)(2,1)S(1)} %get-tuple-element.14), channel_id=1, source_target_pairs={{0,1},{1,2},{2,3},{4,5},{5,6},{6,7},{8,9},{9,10},{10,11},{12,13},{... | collective-permute-start | bytes 6152 | tf_op jit(solution)/shard_map/ppermute | solution.py:17
  72.5 0.2 convolution_subtract_fusion.1
  72.7 0.6 collective-permute-done.10
  73.3 1.0 fusion.83
  74.3 3.9 %gather_fusion = bf16[1024,256]{1,0:T(8,128)(2,1)S(1)} fusion(bf16[128,256]{1,0:T(8,128)(2,1)S(1)} %bitcast.84, s32[1024]{0:T(1024)S(1)} %broadcast_clamp_fusion.1), kind=kCustom, calls=%fused_computation | custom fusion | bytes 1052672 | tf_op jit(solution)/shard_map/jit(_take)/gather | solution.py:84
  78.3 0.9 fusion.11
  79.2 6.5 %all-to-all-start.1 = ((f32[4,3,256]{2,1,0:T(4,128)}), f32[4,3,256]{2,1,0:T(4,128)S(1)}, u32[]{:S(2)}, u32[]{:S(2)}) async-start(f32[4,3,256]{2,1,0:T(4,128)} %fusion.11), calls=%async_computation.1 | async-start | bytes 32768 | tf_op jit(solution)/shard_map/all_to_all | solution.py:96
  85.7 3.8 %all-to-all-done.1 = f32[4,3,256]{2,1,0:T(4,128)S(1)} async-done(((f32[4,3,256]{2,1,0:T(4,128)}), f32[4,3,256]{2,1,0:T(4,128)S(1)}, u32[]{:S(2)}, u32[]{:S(2)}) %all-to-all-start.1) | async-done | bytes 12320 | tf_op jit(solution)/shard_map/all_to_all | solution.py:96
  89.5 0.2 copy.23
  89.8 0.0 copy-start.3
  89.8 0.0 copy-start.5
  89.8 8.2 %scatter_custom_fusion = f32[3,8192]{0,1:T(8,128)} fusion(s32[1024]{0:T(1024)S(1)} %bitcast.95, f32[1024,3]{1,0:T(8,128)S(1)} %copy.23, f32[]{:T(128)} %constant.9.clone.1), kind=kCustom, calls=%fused_computation.3 | custom fusion | flops 3072 | bytes 98308 | tf_op jit(solution)/shard_map/scatter-add | solution.py:100
  98.0 3.5 %copy.24 = f32[3,64,128]{2,1,0:T(8,128)} copy(f32[3,64,128]{0,2,1:T(8,128)} %bitcast.86) | data formatting | bytes 196608 | tf_op jit(solution)/shard_map/reshape | solution.py:102
  101.5 0.0 all-reduce.4.cloned.1.call-update
  101.6 73.6 %all-reduce.4.cloned.1.call-done = f32[3,64,128]{2,1,0:T(8,128)} async-done(((f32[3,64,128]{2,1,0:T(8,128)}), f32[3,64,128]{2,1,0:T(8,128)}) %all-reduce.4.cloned.1.call-update) | async-done | bytes 98320 | tf_op jit(solution)/shard_map/psum | solution.py:101
  175.2 1.0 fusion.33
  176.2 2.6 copy.25
  178.8 103.9 %all_gather.3 = f32[3,32768]{0,1:T(8,128)} all-gather(f32[3,8192]{0,1:T(8,128)} %bitcast.85), channel_id=1, replica_groups=mesh['slab'=8,'patch'=4] {'patch'}, dimensions={1}, use_global_device_ids=true | all-gather | bytes 491520 | tf_op jit(solution)/shard_map/all_gather | solution.py:107
  282.7 8.6 %gather_fusion.1 = f32[1024,3]{1,0:T(8,128)S(1)} fusion(f32[3,32768]{0,1:T(8,128)} %all_gather.3, s32[1024]{0:T(1024)S(1)} %broadcast_clamp_fusion), kind=kCustom, calls=%fused_computation.1 | custom fusion | bytes 28672 | tf_op jit(solution)/shard_map/gather | solution.py:108
  291.3 0.2 bitcast_multiply_fusion
  291.5 0.8 copy.26
  (42 shorter events, 0.2 us)
Async XLA Ops:
  7.2 35.8 %copy-start = (bf16[256,256]{1,0:T(8,128)(2,1)S(1)}, bf16[256,256]{1,0:T(8,128)(2,1)}, u32[]{:S(2)}) copy-start(bf16[256,256]{1,0:T(8,128)(2,1)} %param.19) | copy-start | bytes 393220
  7.2 51.1 %copy-start.6 = (f32[2,64]{1,0:T(2,128)S(1)}, f32[2,64]{1,0:T(2,128)}, u32[]{:S(2)}) copy-start(f32[2,64]{1,0:T(2,128)} %param.15) | copy-start | bytes 1540
  7.2 57.9 %copy-start.1 = (bf16[256,256]{1,0:T(8,128)(2,1)S(1)}, bf16[256,256]{1,0:T(8,128)(2,1)}, u32[]{:S(2)}) copy-start(bf16[256,256]{1,0:T(8,128)(2,1)} %param.16) | copy-start | bytes 393220
  7.2 50.3 %copy-start.2 = (bf16[256,256]{1,0:T(8,128)(2,1)S(1)}, bf16[256,256]{1,0:T(8,128)(2,1)}, u32[]{:S(2)}) copy-start(bf16[256,256]{1,0:T(8,128)(2,1)} %param.17) | copy-start | bytes 393220
  7.2 51.1 %copy-start.7 = (f32[2,64,256]{2,1,0:T(8,128)S(1)}, f32[2,64,256]{2,1,0:T(8,128)}, u32[]{:S(2)}) copy-start(f32[2,64,256]{2,1,0:T(8,128)} %param.14) | copy-start | bytes 393220
  7.2 51.1 %copy-start.8 = (bf16[256,256]{1,0:T(8,128)(2,1)S(1)}, bf16[256,256]{1,0:T(8,128)(2,1)}, u32[]{:S(2)}) copy-start(bf16[256,256]{1,0:T(8,128)(2,1)} %param.18) | copy-start | bytes 393220
  8.3 28.0 %collective-permute-start.1 = (bf16[1,64,256]{2,1,0:T(8,128)(2,1)S(1)}, bf16[1,64,256]{2,1,0:T(8,128)(2,1)S(1)}, u32[]{:S(2)}, u32[]{:S(2)}) collective-permute-start(bf16[1,64,256]{2,1,0:T(8,128)(2,1)S(1)} %get-tuple-element.25), channel_id=1, source_target_pairs={{4,0},{8,4},{12,8},{16,12},{20,16},{24,20},{28,24},{5,1},{9,5},{13... | collective-permute-start | bytes 98312 | tf_op jit(solution)/shard_map/ppermute | solution.py:19
  9.6 26.7 %collective-permute-start = (bf16[1,64,256]{2,1,0:T(8,128)(2,1)S(1)}, bf16[1,64,256]{2,1,0:T(8,128)(2,1)S(1)}, u32[]{:S(2)}, u32[]{:S(2)}) collective-permute-start(bf16[1,64,256]{2,1,0:T(8,128)(2,1)S(1)} %get-tuple-element.24), channel_id=1, source_target_pairs={{0,4},{4,8},{8,12},{12,16},{16,20},{20,24},{24,28},{1,5},{5,9},{9,... | collective-permute-start | bytes 98312 | tf_op jit(solution)/shard_map/ppermute | solution.py:17
  15.1 64.1 %all-to-all-start = ((s32[4,1,256]{2,1,0:T(1,128)}), s32[4,1,256]{2,1,0:T(1,128)S(1)}, u32[]{:S(2)}, u32[]{:S(2)}) async-start(s32[4,1,256]{2,1,0:T(1,128)} %bitcast.90), calls=%async_computation | async-start | bytes 8192 | tf_op jit(solution)/shard_map/all_to_all | solution.py:97
  19.3 10.3 %collective-permute-start.13 = (bf16[3,1,128]{2,1,0:T(2,128)(2,1)S(1)}, bf16[3,1,128]{2,1,0:T(2,128)(2,1)S(1)}, u32[]{:S(2)}, u32[]{:S(2)}) collective-permute-start(bf16[3,1,128]{2,1,0:T(2,128)(2,1)S(1)} %get-tuple-element.29), channel_id=1, source_target_pairs={{1,0},{2,1},{3,2},{5,4},{6,5},{7,6},{9,8},{10,9},{11,10},{13,12},{... | collective-permute-start | bytes 2312 | tf_op jit(solution)/shard_map/ppermute | solution.py:19
  20.6 9.0 %collective-permute-start.12 = (bf16[3,1,128]{2,1,0:T(2,128)(2,1)S(1)}, bf16[3,1,128]{2,1,0:T(2,128)(2,1)S(1)}, u32[]{:S(2)}, u32[]{:S(2)}) collective-permute-start(bf16[3,1,128]{2,1,0:T(2,128)(2,1)S(1)} %get-tuple-element.28), channel_id=1, source_target_pairs={{0,1},{1,2},{2,3},{4,5},{5,6},{6,7},{8,9},{9,10},{10,11},{12,13},{... | collective-permute-start | bytes 2312 | tf_op jit(solution)/shard_map/ppermute | solution.py:17
  30.7 70.8 %collective-permute-start.15 = (bf16[3,1,128]{2,1,0:T(2,128)(2,1)S(1)}, bf16[3,1,128]{2,1,0:T(2,128)(2,1)S(1)}, u32[]{:S(2)}, u32[]{:S(2)}) collective-permute-start(bf16[3,1,128]{2,1,0:T(2,128)(2,1)S(1)} %get-tuple-element.27), channel_id=1, source_target_pairs={{1,0},{2,1},{3,2},{5,4},{6,5},{7,6},{9,8},{10,9},{11,10},{13,12},{... | collective-permute-start | bytes 2312 | tf_op jit(solution)/shard_map/ppermute | solution.py:19
  32.0 69.6 %collective-permute-start.14 = (bf16[3,1,128]{2,1,0:T(2,128)(2,1)S(1)}, bf16[3,1,128]{2,1,0:T(2,128)(2,1)S(1)}, u32[]{:S(2)}, u32[]{:S(2)}) collective-permute-start(bf16[3,1,128]{2,1,0:T(2,128)(2,1)S(1)} %get-tuple-element.26), channel_id=1, source_target_pairs={{0,1},{1,2},{2,3},{4,5},{5,6},{6,7},{8,9},{9,10},{10,11},{12,13},{... | collective-permute-start | bytes 2312 | tf_op jit(solution)/shard_map/ppermute | solution.py:17
  36.3 6.7 %collective-permute-start.3 = (bf16[4,1,256]{2,1,0:T(2,128)(2,1)S(1)}, bf16[4,1,256]{2,1,0:T(2,128)(2,1)S(1)}, u32[]{:S(2)}, u32[]{:S(2)}) collective-permute-start(bf16[4,1,256]{2,1,0:T(2,128)(2,1)S(1)} %get-tuple-element.19), channel_id=1, source_target_pairs={{1,0},{2,1},{3,2},{5,4},{6,5},{7,6},{9,8},{10,9},{11,10},{13,12},{... | collective-permute-start | bytes 6152 | tf_op jit(solution)/shard_map/ppermute | solution.py:19
  37.6 5.4 %collective-permute-start.2 = (bf16[4,1,256]{2,1,0:T(2,128)(2,1)S(1)}, bf16[4,1,256]{2,1,0:T(2,128)(2,1)S(1)}, u32[]{:S(2)}, u32[]{:S(2)}) collective-permute-start(bf16[4,1,256]{2,1,0:T(2,128)(2,1)S(1)} %get-tuple-element.18), channel_id=1, source_target_pairs={{0,1},{1,2},{2,3},{4,5},{5,6},{6,7},{8,9},{9,10},{10,11},{12,13},{... | collective-permute-start | bytes 6152 | tf_op jit(solution)/shard_map/ppermute | solution.py:17
  44.3 7.8 %collective-permute-start.5 = (bf16[1,64,256]{2,1,0:T(8,128)(2,1)S(1)}, bf16[1,64,256]{2,1,0:T(8,128)(2,1)S(1)}, u32[]{:S(2)}, u32[]{:S(2)}) collective-permute-start(bf16[1,64,256]{2,1,0:T(8,128)(2,1)S(1)} %get-tuple-element.23), channel_id=1, source_target_pairs={{4,0},{8,4},{12,8},{16,12},{20,16},{24,20},{28,24},{5,1},{9,5},{13... | collective-permute-start | bytes 98312 | tf_op jit(solution)/shard_map/ppermute | solution.py:19
  45.6 7.0 %collective-permute-start.4 = (bf16[1,64,256]{2,1,0:T(8,128)(2,1)S(1)}, bf16[1,64,256]{2,1,0:T(8,128)(2,1)S(1)}, u32[]{:S(2)}, u32[]{:S(2)}) collective-permute-start(bf16[1,64,256]{2,1,0:T(8,128)(2,1)S(1)} %get-tuple-element.22), channel_id=1, source_target_pairs={{0,4},{4,8},{8,12},{12,16},{16,20},{20,24},{24,28},{1,5},{5,9},{9,... | collective-permute-start | bytes 98312 | tf_op jit(solution)/shard_map/ppermute | solution.py:17
  52.6 5.0 %collective-permute-start.7 = (bf16[4,1,256]{2,1,0:T(2,128)(2,1)S(1)}, bf16[4,1,256]{2,1,0:T(2,128)(2,1)S(1)}, u32[]{:S(2)}, u32[]{:S(2)}) collective-permute-start(bf16[4,1,256]{2,1,0:T(2,128)(2,1)S(1)} %get-tuple-element.17), channel_id=1, source_target_pairs={{1,0},{2,1},{3,2},{5,4},{6,5},{7,6},{9,8},{10,9},{11,10},{13,12},{... | collective-permute-start | bytes 6152 | tf_op jit(solution)/shard_map/ppermute | solution.py:19
  53.9 4.3 %collective-permute-start.6 = (bf16[4,1,256]{2,1,0:T(2,128)(2,1)S(1)}, bf16[4,1,256]{2,1,0:T(2,128)(2,1)S(1)}, u32[]{:S(2)}, u32[]{:S(2)}) collective-permute-start(bf16[4,1,256]{2,1,0:T(2,128)(2,1)S(1)} %get-tuple-element.16), channel_id=1, source_target_pairs={{0,1},{1,2},{2,3},{4,5},{5,6},{6,7},{8,9},{9,10},{10,11},{12,13},{... | collective-permute-start | bytes 6152 | tf_op jit(solution)/shard_map/ppermute | solution.py:17
  57.6 20.6 %copy-start.9 = (bf16[3,256]{1,0:T(4,128)(2,1)S(1)}, bf16[3,256]{1,0:T(4,128)(2,1)}, u32[]{:S(2)}) copy-start(bf16[3,256]{1,0:T(4,128)(2,1)} %param.20) | copy-start | bytes 4612
  58.6 6.7 %collective-permute-start.9 = (bf16[1,64,256]{2,1,0:T(8,128)(2,1)S(1)}, bf16[1,64,256]{2,1,0:T(8,128)(2,1)S(1)}, u32[]{:S(2)}, u32[]{:S(2)}) collective-permute-start(bf16[1,64,256]{2,1,0:T(8,128)(2,1)S(1)} %get-tuple-element.21), channel_id=1, source_target_pairs={{4,0},{8,4},{12,8},{16,12},{20,16},{24,20},{28,24},{5,1},{9,5},{13... | collective-permute-start | bytes 98312 | tf_op jit(solution)/shard_map/ppermute | solution.py:19
  59.9 6.8 %collective-permute-start.8 = (bf16[1,64,256]{2,1,0:T(8,128)(2,1)S(1)}, bf16[1,64,256]{2,1,0:T(8,128)(2,1)S(1)}, u32[]{:S(2)}, u32[]{:S(2)}) collective-permute-start(bf16[1,64,256]{2,1,0:T(8,128)(2,1)S(1)} %get-tuple-element.20), channel_id=1, source_target_pairs={{0,4},{4,8},{8,12},{12,16},{16,20},{20,24},{24,28},{1,5},{5,9},{9,... | collective-permute-start | bytes 98312 | tf_op jit(solution)/shard_map/ppermute | solution.py:17
  66.7 6.0 %collective-permute-start.11 = (bf16[4,1,256]{2,1,0:T(2,128)(2,1)S(1)}, bf16[4,1,256]{2,1,0:T(2,128)(2,1)S(1)}, u32[]{:S(2)}, u32[]{:S(2)}) collective-permute-start(bf16[4,1,256]{2,1,0:T(2,128)(2,1)S(1)} %get-tuple-element.15), channel_id=1, source_target_pairs={{1,0},{2,1},{3,2},{5,4},{6,5},{7,6},{9,8},{10,9},{11,10},{13,12},{... | collective-permute-start | bytes 6152 | tf_op jit(solution)/shard_map/ppermute | solution.py:19
  68.0 5.4 %collective-permute-start.10 = (bf16[4,1,256]{2,1,0:T(2,128)(2,1)S(1)}, bf16[4,1,256]{2,1,0:T(2,128)(2,1)S(1)}, u32[]{:S(2)}, u32[]{:S(2)}) collective-permute-start(bf16[4,1,256]{2,1,0:T(2,128)(2,1)S(1)} %get-tuple-element.14), channel_id=1, source_target_pairs={{0,1},{1,2},{2,3},{4,5},{5,6},{6,7},{8,9},{9,10},{10,11},{12,13},{... | collective-permute-start | bytes 6152 | tf_op jit(solution)/shard_map/ppermute | solution.py:17
  79.2 10.4 %all-to-all-start.1 = ((f32[4,3,256]{2,1,0:T(4,128)}), f32[4,3,256]{2,1,0:T(4,128)S(1)}, u32[]{:S(2)}, u32[]{:S(2)}) async-start(f32[4,3,256]{2,1,0:T(4,128)} %fusion.11), calls=%async_computation.1 | async-start | bytes 32768 | tf_op jit(solution)/shard_map/all_to_all | solution.py:96
  85.7 89.5 %all-reduce.4.cloned.1.call-start = ((), (), s32[]{:S(2)}) async-start(), calls=%async_computation.2 | async-start | bytes 196608 | tf_op jit(solution)/shard_map/psum | solution.py:101
  89.8 85.4 %copy-start.3 = (f32[3,64,128]{2,1,0:T(8,128)S(1)}, f32[3,64,128]{2,1,0:T(8,128)}, u32[]{:S(2)}) copy-start(f32[3,64,128]{2,1,0:T(8,128)} %param.24) | copy-start | bytes 294916
  89.8 85.4 %copy-start.5 = (f32[64,128]{1,0:T(8,128)S(1)}, f32[64,128]{1,0:T(8,128)}, u32[]{:S(2)}) copy-start(f32[64,128]{1,0:T(8,128)} %param.25) | copy-start | bytes 98308
  176.2 106.5 %copy-start.4 = (f32[3,64,128]{2,1,0:T(8,128)}, f32[3,64,128]{2,1,0:T(8,128)S(1)}, u32[]{:S(2)}) copy-start(f32[3,64,128]{2,1,0:T(8,128)S(1)} %fusion.33) | copy-start | bytes 294916
Sparse Core Ops, SparseCore 0:
  101.6 73.4 all-reduce.3
where the time goes:
time: 300 us; the launch traced here: 299 us
  blocking collectives  104 us (35%)
  waiting for transfers between devices  80.6 us (27%)
  starting transfers between devices  55.9 us (19%)
  local copies, waits for them, and re-layouts  20.3 us (7%)
  other arithmetic  16.7 us (6%)
  between operations  14.5 us (5%)
  matrix products  7.25 us (2%)
    all_gather x1, blocking collectives, shards(): whole = lax.all_gather(flat_net, 'patch', axis=1, tiled=True)  104 us
    psum x1, waiting for transfers between devices, shards(): loads = lax.psum(local, 'slab')  73.6 us
    ppermute x8, starting transfers between devices, with_halo(): lax.ppermute(tail, axis, [(i, (i + 1) % count) for i in range(ends)])  35.8 us
    ppermute x8, starting transfers between devices, with_halo(): lax.ppermute(head, axis, [((i + 1) % count, i) for i in range(ends)])  10.3 us
    gather x1, local copies, waits for them, and re-layouts, shards(): picked = whole[:, (owner_ids * cells + points).reshape(-1)]  8.57 us
    scatter-add x1, other arithmetic, shards(): local.at[:, got_points.reshape(-1)]  8.21 us
    all_to_all x1, starting transfers between devices, shards(): lax.all_to_all(pull, 'patch', split_axis=0, concat_axis=0, tiled=True)  6.5 us
  transfers between devices with their start and end apart: 19, of which 6 were waited for; matrix products, arithmetic and copies ran while one was open for 10% of the time, Pallas kernels for 0%

commit v1 on v0

--- a/solution.py
+++ b/solution.py
@@ -104,7 +104,14 @@
     stiff_term = stiffness[None] * (laplace_net(bend) + 4.0 * bend)
     displacement_new = displacement + (loads - stiff_term) / (36.0 * stiffness[None])
     flat_net = displacement_new.reshape(3, -1)
-    whole = lax.all_gather(flat_net, "patch", axis=1, tiled=True)
+    ring = [flat_net]
+    for hop in range(3):
+        ring.append(lax.ppermute(ring[-1], "patch", [(dev, (dev + 1) % 4) for dev in range(4)]))
+    whole = jnp.roll(
+        jnp.concatenate(ring[::-1], axis=1),
+        (lax.axis_index("patch") + 1) * ring[0].shape[1],
+        axis=1,
+    )
     picked = whole[:, (owner_ids * cells + points).reshape(-1)]
     wall_motion = (picked * live.reshape(1, -1)).reshape(3, 1, 1, owners * capacity)
     return (state, displacement_new, wall_motion)

time: 300 us -> 216 us (0.72)
  blocking collectives: 104 us -> 0 us
  waiting for transfers between devices: 80.6 us -> 102 us
  starting transfers between devices: 55.9 us -> 48.5 us
  local copies, waits for them, and re-layouts: 20.3 us -> 26.7 us
    all_gather x1 -> x0, blocking collectives: 104 us -> none  [shards(): whole = lax.all_gather(flat_net, 'patch', axis=1, tiled=True)]
    ppermute x8, waiting for transfers between devices: 0.02 us -> 14.8 us  [with_halo(): lax.ppermute(head, axis, [((i + 1) % count, i) for i in range(ends)])]
    ppermute x0 -> x3, waiting for transfers between devices: none -> 13.2 us  [shards(): lax.ppermute(ring[-1], 'patch', [(dev, (dev + 1) % 4) for dev in range(4)])]
    unnamed x25 -> x34, local copies, waits for them, and re-layouts: 1.45 us -> 10.3 us
    ppermute x8, starting transfers between devices: 35.8 us -> 30.1 us  [with_halo(): lax.ppermute(tail, axis, [(i, (i + 1) % count) for i in range(ends)])]
    psum x1, waiting for transfers between devices: 73.6 us -> 69.7 us  [shards(): loads = lax.psum(local, 'slab')]
    ppermute x8, waiting for transfers between devices: 3.13 us -> 0.12 us  [with_halo(): lax.ppermute(tail, axis, [(i, (i + 1) % count) for i in range(ends)])]
  transfers between devices with their start and end apart: 19 -> 22, of which waited for: 6 -> 11; matrix products, arithmetic and copies ran while one was open for 10% -> 14% of each run, Pallas kernels for 0% -> 0%
where the time goes in v1:
time: 216 us; the launch traced here: 215 us
  waiting for transfers between devices  102 us (47%)
  starting transfers between devices  48.5 us (22%)
  local copies, waits for them, and re-layouts  26.7 us (12%)
  other arithmetic  16.6 us (8%)
  between operations  14.6 us (7%)
  matrix products  7.24 us (3%)
    psum x1, waiting for transfers between devices, shards(): loads = lax.psum(local, 'slab')  69.7 us
    ppermute x8, starting transfers between devices, with_halo(): lax.ppermute(tail, axis, [(i, (i + 1) % count) for i in range(ends)])  30.1 us
    ppermute x8, waiting for transfers between devices, with_halo(): lax.ppermute(head, axis, [((i + 1) % count, i) for i in range(ends)])  14.8 us
    ppermute x3, waiting for transfers between devices, shards(): lax.ppermute(ring[-1], 'patch', [(dev, (dev + 1) % 4) for dev in range(4)])  13.2 us
    ppermute x8, starting transfers between devices, with_halo(): lax.ppermute(head, axis, [((i + 1) % count, i) for i in range(ends)])  10.3 us
    unnamed x34, local copies, waits for them, and re-layouts  10.3 us
    gather x1, local copies, waits for them, and re-layouts, shards(): picked = whole[:, (owner_ids * cells + points).reshape(-1)]  8.57 us
    scatter-add x1, other arithmetic, shards(): local.at[:, got_points.reshape(-1)]  8.21 us
  transfers between devices with their start and end apart: 22, of which 11 were waited for; matrix products, arithmetic and copies ran while one was open for 14% of the time, Pallas kernels for 0%

profile of v1, /device:TPU:0, one launch (start us, length us, event | category | flops | bytes accessed | tf_op | source)
XLA Modules:
  0.0 215.1 jit_solution(13950797148802453347)
XLA Ops:
  7.2 4.4 %all-to-all-start = ((s32[4,1,256]{2,1,0:T(1,128)}), s32[4,1,256]{2,1,0:T(1,128)S(1)}, u32[]{:S(2)}, u32[]{:S(2)}) async-start(s32[4,1,256]{2,1,0:T(1,128)} %bitcast.100), calls=%async_computation | async-start | bytes 8192 | tf_op jit(solution)/shard_map/all_to_all | solution.py:97
  11.6 0.9 convert_element_type.132
  12.5 2.4 %collective-permute-start.12 = (bf16[3,1,128]{2,1,0:T(2,128)(2,1)S(1)}, bf16[3,1,128]{2,1,0:T(2,128)(2,1)S(1)}, u32[]{:S(2)}, u32[]{:S(2)}) collective-permute-start(bf16[3,1,128]{2,1,0:T(2,128)(2,1)S(1)} %get-tuple-element.28), channel_id=1, source_target_pairs={{0,1},{1,2},{2,3},{4,5},{5,6},{6,7},{8,9},{9,10},{10,11},{12,13},{... | collective-permute-start | bytes 2312 | tf_op jit(solution)/shard_map/ppermute | solution.py:17
  14.9 1.3 collective-permute-start.13
  16.2 0.9 convert_element_type.106
  17.2 3.9 %collective-permute-start = (bf16[1,64,256]{2,1,0:T(8,128)(2,1)S(1)}, bf16[1,64,256]{2,1,0:T(8,128)(2,1)S(1)}, u32[]{:S(2)}, u32[]{:S(2)}) collective-permute-start(bf16[1,64,256]{2,1,0:T(8,128)(2,1)S(1)} %get-tuple-element.24), channel_id=1, source_target_pairs={{0,4},{4,8},{8,12},{12,16},{16,20},{20,24},{24,28},{1,5},{5,9},{9,... | collective-permute-start | bytes 98312 | tf_op jit(solution)/shard_map/ppermute | solution.py:17
  21.1 1.3 collective-permute-start.1
  22.4 0.1 broadcast_bitcast_fusion
  22.5 0.7 compare_select_fusion
  23.1 0.7 compare_select_fusion.1
  23.8 0.5 broadcast.127
  24.4 1.3 reduce.3
  25.7 0.8 broadcast_multiply_fusion
  26.5 1.1 convolution_multiply_fusion.2
  27.6 0.7 fusion.59
  28.3 1.0 fusion.70
  29.4 3.9 %collective-permute-start.14 = (bf16[3,1,128]{2,1,0:T(2,128)(2,1)S(1)}, bf16[3,1,128]{2,1,0:T(2,128)(2,1)S(1)}, u32[]{:S(2)}, u32[]{:S(2)}) collective-permute-start(bf16[3,1,128]{2,1,0:T(2,128)(2,1)S(1)} %get-tuple-element.26), channel_id=1, source_target_pairs={{0,1},{1,2},{2,3},{4,5},{5,6},{6,7},{8,9},{9,10},{10,11},{12,13},{... | collective-permute-start | bytes 2312 | tf_op jit(solution)/shard_map/ppermute | solution.py:17
  33.2 1.3 collective-permute-start.15
  34.6 4.6 %collective-permute-start.2 = (bf16[4,1,256]{2,1,0:T(2,128)(2,1)S(1)}, bf16[4,1,256]{2,1,0:T(2,128)(2,1)S(1)}, u32[]{:S(2)}, u32[]{:S(2)}) collective-permute-start(bf16[4,1,256]{2,1,0:T(2,128)(2,1)S(1)} %get-tuple-element.18), channel_id=1, source_target_pairs={{0,1},{1,2},{2,3},{4,5},{5,6},{6,7},{8,9},{9,10},{10,11},{12,13},{... | collective-permute-start | bytes 6152 | tf_op jit(solution)/shard_map/ppermute | solution.py:17
  39.1 1.3 collective-permute-start.3
  40.4 1.1 convolution_subtract_fusion.5
  41.5 1.9 collective-permute-done.3
  43.5 1.3 fusion.77
  44.8 4.5 %collective-permute-start.4 = (bf16[1,64,256]{2,1,0:T(8,128)(2,1)S(1)}, bf16[1,64,256]{2,1,0:T(8,128)(2,1)S(1)}, u32[]{:S(2)}, u32[]{:S(2)}) collective-permute-start(bf16[1,64,256]{2,1,0:T(8,128)(2,1)S(1)} %get-tuple-element.22), channel_id=1, source_target_pairs={{0,4},{4,8},{8,12},{12,16},{16,20},{20,24},{24,28},{1,5},{5,9},{9,... | collective-permute-start | bytes 98312 | tf_op jit(solution)/shard_map/ppermute | solution.py:17
  49.4 1.3 collective-permute-start.5
  50.7 1.1 convolution_multiply_fusion.1
  51.8 3.8 %collective-permute-done.5 = bf16[1,64,256]{2,1,0:T(8,128)(2,1)S(1)} collective-permute-done((bf16[1,64,256]{2,1,0:T(8,128)(2,1)S(1)}, bf16[1,64,256]{2,1,0:T(8,128)(2,1)S(1)}, u32[]{:S(2)}, u32[]{:S(2)}) %collective-permute-start.5) | collective-permute-done | bytes 32800 | tf_op jit(solution)/shard_map/ppermute | solution.py:19
  55.6 3.1 %collective-permute-start.6 = (bf16[4,1,256]{2,1,0:T(2,128)(2,1)S(1)}, bf16[4,1,256]{2,1,0:T(2,128)(2,1)S(1)}, u32[]{:S(2)}, u32[]{:S(2)}) collective-permute-start(bf16[4,1,256]{2,1,0:T(2,128)(2,1)S(1)} %get-tuple-element.16), channel_id=1, source_target_pairs={{0,1},{1,2},{2,3},{4,5},{5,6},{6,7},{8,9},{9,10},{10,11},{12,13},{... | collective-permute-start | bytes 6152 | tf_op jit(solution)/shard_map/ppermute | solution.py:17
  58.7 1.3 collective-permute-start.7
  60.0 0.2 convolution_subtract_fusion.3
  60.2 2.3 %collective-permute-done.7 = bf16[4,1,256]{2,1,0:T(2,128)(2,1)S(1)} collective-permute-done((bf16[4,1,256]{2,1,0:T(2,128)(2,1)S(1)}, bf16[4,1,256]{2,1,0:T(2,128)(2,1)S(1)}, u32[]{:S(2)}, u32[]{:S(2)}) %collective-permute-start.7) | collective-permute-done | bytes 2080 | tf_op jit(solution)/shard_map/ppermute | solution.py:19
  62.5 0.3 fusion.80
  62.8 4.8 %collective-permute-start.8 = (bf16[1,64,256]{2,1,0:T(8,128)(2,1)S(1)}, bf16[1,64,256]{2,1,0:T(8,128)(2,1)S(1)}, u32[]{:S(2)}, u32[]{:S(2)}) collective-permute-start(bf16[1,64,256]{2,1,0:T(8,128)(2,1)S(1)} %get-tuple-element.20), channel_id=1, source_target_pairs={{0,4},{4,8},{8,12},{12,16},{16,20},{20,24},{24,28},{1,5},{5,9},{9,... | collective-permute-start | bytes 98312 | tf_op jit(solution)/shard_map/ppermute | solution.py:17
  67.7 1.3 collective-permute-start.9
  69.0 0.2 convolution_multiply_fusion
  69.1 0.1 collective-permute-done.8
  69.2 4.2 %collective-permute-done.9 = bf16[1,64,256]{2,1,0:T(8,128)(2,1)S(1)} collective-permute-done((bf16[1,64,256]{2,1,0:T(8,128)(2,1)S(1)}, bf16[1,64,256]{2,1,0:T(8,128)(2,1)S(1)}, u32[]{:S(2)}, u32[]{:S(2)}) %collective-permute-start.9) | collective-permute-done | bytes 32800 | tf_op jit(solution)/shard_map/ppermute | solution.py:19
  73.5 2.8 %collective-permute-start.10 = (bf16[4,1,256]{2,1,0:T(2,128)(2,1)S(1)}, bf16[4,1,256]{2,1,0:T(2,128)(2,1)S(1)}, u32[]{:S(2)}, u32[]{:S(2)}) collective-permute-start(bf16[4,1,256]{2,1,0:T(2,128)(2,1)S(1)} %get-tuple-element.14), channel_id=1, source_target_pairs={{0,1},{1,2},{2,3},{4,5},{5,6},{6,7},{8,9},{9,10},{10,11},{12,13},{... | collective-permute-start | bytes 6152 | tf_op jit(solution)/shard_map/ppermute | solution.py:17
  76.3 1.3 collective-permute-start.11
  77.6 0.2 convolution_subtract_fusion.1
  77.8 2.6 %collective-permute-done.11 = bf16[4,1,256]{2,1,0:T(2,128)(2,1)S(1)} collective-permute-done((bf16[4,1,256]{2,1,0:T(2,128)(2,1)S(1)}, bf16[4,1,256]{2,1,0:T(2,128)(2,1)S(1)}, u32[]{:S(2)}, u32[]{:S(2)}) %collective-permute-start.11) | collective-permute-done | bytes 2080 | tf_op jit(solution)/shard_map/ppermute | solution.py:19
  80.4 1.0 fusion.83
  81.3 3.9 %gather_fusion = bf16[1024,256]{1,0:T(8,128)(2,1)S(1)} fusion(bf16[128,256]{1,0:T(8,128)(2,1)S(1)} %bitcast.91, s32[1024]{0:T(1024)S(1)} %get-tuple-element.39), kind=kCustom, calls=%fused_computation | custom fusion | bytes 1052672 | tf_op jit(solution)/shard_map/jit(_take)/gather | solution.py:84
  85.3 0.9 fusion.11
  86.2 3.6 %all-to-all-start.1 = ((f32[4,3,256]{2,1,0:T(4,128)}), f32[4,3,256]{2,1,0:T(4,128)S(1)}, u32[]{:S(2)}, u32[]{:S(2)}) async-start(f32[4,3,256]{2,1,0:T(4,128)} %fusion.11), calls=%async_computation.1 | async-start | bytes 32768 | tf_op jit(solution)/shard_map/all_to_all | solution.py:96
  89.9 3.8 %all-to-all-done.1 = f32[4,3,256]{2,1,0:T(4,128)S(1)} async-done(((f32[4,3,256]{2,1,0:T(4,128)}), f32[4,3,256]{2,1,0:T(4,128)S(1)}, u32[]{:S(2)}, u32[]{:S(2)}) %all-to-all-start.1) | async-done | bytes 12320 | tf_op jit(solution)/shard_map/all_to_all | solution.py:96
  93.7 0.2 copy.23
  94.0 8.2 %scatter_custom_fusion = f32[3,8192]{0,1:T(8,128)} fusion(s32[1024]{0:T(1024)S(1)} %bitcast.105, f32[1024,3]{1,0:T(8,128)S(1)} %copy.23, f32[]{:T(128)} %constant.27.clone.1), kind=kCustom, calls=%fused_computation.3 | custom fusion | flops 3072 | bytes 98308 | tf_op jit(solution)/shard_map/scatter-add | solution.py:100
  102.2 3.5 %copy.24 = f32[3,64,128]{2,1,0:T(8,128)} copy(f32[3,64,128]{0,2,1:T(8,128)} %bitcast.92) | data formatting | bytes 196608 | tf_op jit(solution)/shard_map/reshape | solution.py:102
  105.6 0.0 all-reduce.4.cloned.1.call-update
  105.7 69.7 %all-reduce.4.cloned.1.call-done = f32[3,64,128]{2,1,0:T(8,128)} async-done(((f32[3,64,128]{2,1,0:T(8,128)}), f32[3,64,128]{2,1,0:T(8,128)}) %all-reduce.4.cloned.1.call-update) | async-done | bytes 98320 | tf_op jit(solution)/shard_map/psum | solution.py:101
  175.4 1.0 fusion.33
  176.4 0.1 copy.36
  176.5 0.1 collective-permute-start.16
  176.5 4.4 %collective-permute-done.16 = f32[3,8192]{1,0:T(4,128)S(1)} collective-permute-done((f32[3,8192]{1,0:T(4,128)S(1)}, f32[3,8192]{1,0:T(4,128)S(1)}, u32[]{:S(2)}, u32[]{:S(2)}) %collective-permute-start.16) | collective-permute-done | bytes 98336 | tf_op jit(solution)/shard_map/ppermute | solution.py:109
  180.9 4.4 %collective-permute-done.17 = f32[3,8192]{1,0:T(4,128)S(1)} collective-permute-done((f32[3,8192]{1,0:T(4,128)S(1)}, f32[3,8192]{1,0:T(4,128)S(1)}, u32[]{:S(2)}, u32[]{:S(2)}) %collective-permute-start.17) | collective-permute-done | bytes 98336 | tf_op jit(solution)/shard_map/ppermute | solution.py:109
  185.3 4.4 %collective-permute-done.18 = f32[3,8192]{1,0:T(4,128)S(1)} collective-permute-done((f32[3,8192]{1,0:T(4,128)S(1)}, f32[3,8192]{1,0:T(4,128)S(1)}, u32[]{:S(2)}, u32[]{:S(2)}) %collective-permute-start.18) | collective-permute-done | bytes 98336 | tf_op jit(solution)/shard_map/ppermute | solution.py:109
  189.8 0.1 constant_dynamic-update-slice_fusion.4
  190.0 0.1 constant_dynamic-update-slice_fusion
  190.1 0.1 constant_dynamic-slice_fusion
  190.2 8.5 %copy.27 = f32[3,32768]{0,1:T(8,128)} copy(f32[3,32768]{1,0:T(4,128)S(1)} %constant_dynamic-slice_fusion) | data formatting | bytes 786432
  198.7 8.6 %gather_fusion.1 = f32[1024,3]{1,0:T(8,128)S(1)} fusion(f32[3,32768]{0,1:T(8,128)} %copy.27, s32[1024]{0:T(1024)S(1)} %get-tuple-element.38), kind=kCustom, calls=%fused_computation.1 | custom fusion | bytes 28672 | tf_op jit(solution)/shard_map/gather | solution.py:115
  207.3 0.2 bitcast_multiply_fusion
  207.5 0.8 copy.26
  (56 shorter events, 0.4 us)
Async XLA Ops:
  7.2 36.3 %copy-start = (bf16[256,256]{1,0:T(8,128)(2,1)S(1)}, bf16[256,256]{1,0:T(8,128)(2,1)}, u32[]{:S(2)}) copy-start(bf16[256,256]{1,0:T(8,128)(2,1)} %param.19) | copy-start | bytes 393220
  7.2 55.3 %copy-start.6 = (f32[2,64]{1,0:T(2,128)S(1)}, f32[2,64]{1,0:T(2,128)}, u32[]{:S(2)}) copy-start(f32[2,64]{1,0:T(2,128)} %param.15) | copy-start | bytes 1540
  7.2 61.8 %copy-start.2 = (bf16[256,256]{1,0:T(8,128)(2,1)S(1)}, bf16[256,256]{1,0:T(8,128)(2,1)}, u32[]{:S(2)}) copy-start(bf16[256,256]{1,0:T(8,128)(2,1)} %param.16) | copy-start | bytes 393220
  7.2 52.8 %copy-start.3 = (bf16[256,256]{1,0:T(8,128)(2,1)S(1)}, bf16[256,256]{1,0:T(8,128)(2,1)}, u32[]{:S(2)}) copy-start(bf16[256,256]{1,0:T(8,128)(2,1)} %param.17) | copy-start | bytes 393220
  7.2 55.3 %copy-start.8 = (bf16[256,256]{1,0:T(8,128)(2,1)S(1)}, bf16[256,256]{1,0:T(8,128)(2,1)}, u32[]{:S(2)}) copy-start(bf16[256,256]{1,0:T(8,128)(2,1)} %param.18) | copy-start | bytes 393220
  7.2 55.3 %copy-start.7 = (f32[2,64,256]{2,1,0:T(8,128)S(1)}, f32[2,64,256]{2,1,0:T(8,128)}, u32[]{:S(2)}) copy-start(f32[2,64,256]{2,1,0:T(8,128)} %param.14) | copy-start | bytes 393220
  7.2 79.0 %all-to-all-start = ((s32[4,1,256]{2,1,0:T(1,128)}), s32[4,1,256]{2,1,0:T(1,128)S(1)}, u32[]{:S(2)}, u32[]{:S(2)}) async-start(s32[4,1,256]{2,1,0:T(1,128)} %bitcast.100), calls=%async_computation | async-start | bytes 8192 | tf_op jit(solution)/shard_map/all_to_all | solution.py:97
  12.5 15.8 %collective-permute-start.12 = (bf16[3,1,128]{2,1,0:T(2,128)(2,1)S(1)}, bf16[3,1,128]{2,1,0:T(2,128)(2,1)S(1)}, u32[]{:S(2)}, u32[]{:S(2)}) collective-permute-start(bf16[3,1,128]{2,1,0:T(2,128)(2,1)S(1)} %get-tuple-element.28), channel_id=1, source_target_pairs={{0,1},{1,2},{2,3},{4,5},{5,6},{6,7},{8,9},{9,10},{10,11},{12,13},{... | collective-permute-start | bytes 2312 | tf_op jit(solution)/shard_map/ppermute | solution.py:17
  14.9 13.3 %collective-permute-start.13 = (bf16[3,1,128]{2,1,0:T(2,128)(2,1)S(1)}, bf16[3,1,128]{2,1,0:T(2,128)(2,1)S(1)}, u32[]{:S(2)}, u32[]{:S(2)}) collective-permute-start(bf16[3,1,128]{2,1,0:T(2,128)(2,1)S(1)} %get-tuple-element.29), channel_id=1, source_target_pairs={{1,0},{2,1},{3,2},{5,4},{6,5},{7,6},{9,8},{10,9},{11,10},{13,12},{... | collective-permute-start | bytes 2312 | tf_op jit(solution)/shard_map/ppermute | solution.py:19
  17.2 17.4 %collective-permute-start = (bf16[1,64,256]{2,1,0:T(8,128)(2,1)S(1)}, bf16[1,64,256]{2,1,0:T(8,128)(2,1)S(1)}, u32[]{:S(2)}, u32[]{:S(2)}) collective-permute-start(bf16[1,64,256]{2,1,0:T(8,128)(2,1)S(1)} %get-tuple-element.24), channel_id=1, source_target_pairs={{0,4},{4,8},{8,12},{12,16},{16,20},{20,24},{24,28},{1,5},{5,9},{9,... | collective-permute-start | bytes 98312 | tf_op jit(solution)/shard_map/ppermute | solution.py:17
  21.1 13.5 %collective-permute-start.1 = (bf16[1,64,256]{2,1,0:T(8,128)(2,1)S(1)}, bf16[1,64,256]{2,1,0:T(8,128)(2,1)S(1)}, u32[]{:S(2)}, u32[]{:S(2)}) collective-permute-start(bf16[1,64,256]{2,1,0:T(8,128)(2,1)S(1)} %get-tuple-element.25), channel_id=1, source_target_pairs={{4,0},{8,4},{12,8},{16,12},{20,16},{24,20},{28,24},{5,1},{9,5},{13... | collective-permute-start | bytes 98312 | tf_op jit(solution)/shard_map/ppermute | solution.py:19
  29.4 76.3 %collective-permute-start.14 = (bf16[3,1,128]{2,1,0:T(2,128)(2,1)S(1)}, bf16[3,1,128]{2,1,0:T(2,128)(2,1)S(1)}, u32[]{:S(2)}, u32[]{:S(2)}) collective-permute-start(bf16[3,1,128]{2,1,0:T(2,128)(2,1)S(1)} %get-tuple-element.26), channel_id=1, source_target_pairs={{0,1},{1,2},{2,3},{4,5},{5,6},{6,7},{8,9},{9,10},{10,11},{12,13},{... | collective-permute-start | bytes 2312 | tf_op jit(solution)/shard_map/ppermute | solution.py:17
  33.2 72.4 %collective-permute-start.15 = (bf16[3,1,128]{2,1,0:T(2,128)(2,1)S(1)}, bf16[3,1,128]{2,1,0:T(2,128)(2,1)S(1)}, u32[]{:S(2)}, u32[]{:S(2)}) collective-permute-start(bf16[3,1,128]{2,1,0:T(2,128)(2,1)S(1)} %get-tuple-element.27), channel_id=1, source_target_pairs={{1,0},{2,1},{3,2},{5,4},{6,5},{7,6},{9,8},{10,9},{11,10},{13,12},{... | collective-permute-start | bytes 2312 | tf_op jit(solution)/shard_map/ppermute | solution.py:19
  34.6 6.9 %collective-permute-start.2 = (bf16[4,1,256]{2,1,0:T(2,128)(2,1)S(1)}, bf16[4,1,256]{2,1,0:T(2,128)(2,1)S(1)}, u32[]{:S(2)}, u32[]{:S(2)}) collective-permute-start(bf16[4,1,256]{2,1,0:T(2,128)(2,1)S(1)} %get-tuple-element.18), channel_id=1, source_target_pairs={{0,1},{1,2},{2,3},{4,5},{5,6},{6,7},{8,9},{9,10},{10,11},{12,13},{... | collective-permute-start | bytes 6152 | tf_op jit(solution)/shard_map/ppermute | solution.py:17
  39.1 4.3 %collective-permute-start.3 = (bf16[4,1,256]{2,1,0:T(2,128)(2,1)S(1)}, bf16[4,1,256]{2,1,0:T(2,128)(2,1)S(1)}, u32[]{:S(2)}, u32[]{:S(2)}) collective-permute-start(bf16[4,1,256]{2,1,0:T(2,128)(2,1)S(1)} %get-tuple-element.19), channel_id=1, source_target_pairs={{1,0},{2,1},{3,2},{5,4},{6,5},{7,6},{9,8},{10,9},{11,10},{13,12},{... | collective-permute-start | bytes 6152 | tf_op jit(solution)/shard_map/ppermute | solution.py:19
  44.8 6.9 %collective-permute-start.4 = (bf16[1,64,256]{2,1,0:T(8,128)(2,1)S(1)}, bf16[1,64,256]{2,1,0:T(8,128)(2,1)S(1)}, u32[]{:S(2)}, u32[]{:S(2)}) collective-permute-start(bf16[1,64,256]{2,1,0:T(8,128)(2,1)S(1)} %get-tuple-element.22), channel_id=1, source_target_pairs={{0,4},{4,8},{8,12},{12,16},{16,20},{20,24},{24,28},{1,5},{5,9},{9,... | collective-permute-start | bytes 98312 | tf_op jit(solution)/shard_map/ppermute | solution.py:17
  49.4 6.2 %collective-permute-start.5 = (bf16[1,64,256]{2,1,0:T(8,128)(2,1)S(1)}, bf16[1,64,256]{2,1,0:T(8,128)(2,1)S(1)}, u32[]{:S(2)}, u32[]{:S(2)}) collective-permute-start(bf16[1,64,256]{2,1,0:T(8,128)(2,1)S(1)} %get-tuple-element.23), channel_id=1, source_target_pairs={{4,0},{8,4},{12,8},{16,12},{20,16},{24,20},{28,24},{5,1},{9,5},{13... | collective-permute-start | bytes 98312 | tf_op jit(solution)/shard_map/ppermute | solution.py:19
  55.6 4.6 %collective-permute-start.6 = (bf16[4,1,256]{2,1,0:T(2,128)(2,1)S(1)}, bf16[4,1,256]{2,1,0:T(2,128)(2,1)S(1)}, u32[]{:S(2)}, u32[]{:S(2)}) collective-permute-start(bf16[4,1,256]{2,1,0:T(2,128)(2,1)S(1)} %get-tuple-element.16), channel_id=1, source_target_pairs={{0,1},{1,2},{2,3},{4,5},{5,6},{6,7},{8,9},{9,10},{10,11},{12,13},{... | collective-permute-start | bytes 6152 | tf_op jit(solution)/shard_map/ppermute | solution.py:17
  58.7 3.8 %collective-permute-start.7 = (bf16[4,1,256]{2,1,0:T(2,128)(2,1)S(1)}, bf16[4,1,256]{2,1,0:T(2,128)(2,1)S(1)}, u32[]{:S(2)}, u32[]{:S(2)}) collective-permute-start(bf16[4,1,256]{2,1,0:T(2,128)(2,1)S(1)} %get-tuple-element.17), channel_id=1, source_target_pairs={{1,0},{2,1},{3,2},{5,4},{6,5},{7,6},{9,8},{10,9},{11,10},{13,12},{... | collective-permute-start | bytes 6152 | tf_op jit(solution)/shard_map/ppermute | solution.py:19
  60.2 25.1 %copy-start.9 = (bf16[3,256]{1,0:T(4,128)(2,1)S(1)}, bf16[3,256]{1,0:T(4,128)(2,1)}, u32[]{:S(2)}) copy-start(bf16[3,256]{1,0:T(4,128)(2,1)} %param.20) | copy-start | bytes 4612
  62.8 6.4 %collective-permute-start.8 = (bf16[1,64,256]{2,1,0:T(8,128)(2,1)S(1)}, bf16[1,64,256]{2,1,0:T(8,128)(2,1)S(1)}, u32[]{:S(2)}, u32[]{:S(2)}) collective-permute-start(bf16[1,64,256]{2,1,0:T(8,128)(2,1)S(1)} %get-tuple-element.20), channel_id=1, source_target_pairs={{0,4},{4,8},{8,12},{12,16},{16,20},{20,24},{24,28},{1,5},{5,9},{9,... | collective-permute-start | bytes 98312 | tf_op jit(solution)/shard_map/ppermute | solution.py:17
  67.7 5.8 %collective-permute-start.9 = (bf16[1,64,256]{2,1,0:T(8,128)(2,1)S(1)}, bf16[1,64,256]{2,1,0:T(8,128)(2,1)S(1)}, u32[]{:S(2)}, u32[]{:S(2)}) collective-permute-start(bf16[1,64,256]{2,1,0:T(8,128)(2,1)S(1)} %get-tuple-element.21), channel_id=1, source_target_pairs={{4,0},{8,4},{12,8},{16,12},{20,16},{24,20},{28,24},{5,1},{9,5},{13... | collective-permute-start | bytes 98312 | tf_op jit(solution)/shard_map/ppermute | solution.py:19
  73.5 4.3 %collective-permute-start.10 = (bf16[4,1,256]{2,1,0:T(2,128)(2,1)S(1)}, bf16[4,1,256]{2,1,0:T(2,128)(2,1)S(1)}, u32[]{:S(2)}, u32[]{:S(2)}) collective-permute-start(bf16[4,1,256]{2,1,0:T(2,128)(2,1)S(1)} %get-tuple-element.14), channel_id=1, source_target_pairs={{0,1},{1,2},{2,3},{4,5},{5,6},{6,7},{8,9},{9,10},{10,11},{12,13},{... | collective-permute-start | bytes 6152 | tf_op jit(solution)/shard_map/ppermute | solution.py:17
  76.3 4.0 %collective-permute-start.11 = (bf16[4,1,256]{2,1,0:T(2,128)(2,1)S(1)}, bf16[4,1,256]{2,1,0:T(2,128)(2,1)S(1)}, u32[]{:S(2)}, u32[]{:S(2)}) collective-permute-start(bf16[4,1,256]{2,1,0:T(2,128)(2,1)S(1)} %get-tuple-element.15), channel_id=1, source_target_pairs={{1,0},{2,1},{3,2},{5,4},{6,5},{7,6},{9,8},{10,9},{11,10},{13,12},{... | collective-permute-start | bytes 6152 | tf_op jit(solution)/shard_map/ppermute | solution.py:19
  86.2 7.5 %all-to-all-start.1 = ((f32[4,3,256]{2,1,0:T(4,128)}), f32[4,3,256]{2,1,0:T(4,128)S(1)}, u32[]{:S(2)}, u32[]{:S(2)}) async-start(f32[4,3,256]{2,1,0:T(4,128)} %fusion.11), calls=%async_computation.1 | async-start | bytes 32768 | tf_op jit(solution)/shard_map/all_to_all | solution.py:96
  89.8 85.5 %all-reduce.4.cloned.1.call-start = ((), (), s32[]{:S(2)}) async-start(), calls=%async_computation.2 | async-start | bytes 196608 | tf_op jit(solution)/shard_map/psum | solution.py:101
  93.9 81.4 %copy-start.4 = (f32[3,64,128]{2,1,0:T(8,128)S(1)}, f32[3,64,128]{2,1,0:T(8,128)}, u32[]{:S(2)}) copy-start(f32[3,64,128]{2,1,0:T(8,128)} %param.24) | copy-start | bytes 294916
  93.9 81.4 %copy-start.5 = (f32[64,128]{1,0:T(8,128)S(1)}, f32[64,128]{1,0:T(8,128)}, u32[]{:S(2)}) copy-start(f32[64,128]{1,0:T(8,128)} %param.25) | copy-start | bytes 98308
  176.4 22.3 %copy-start.1 = (f32[3,64,128]{2,1,0:T(8,128)}, f32[3,64,128]{2,1,0:T(8,128)S(1)}, u32[]{:S(2)}) copy-start(f32[3,64,128]{2,1,0:T(8,128)S(1)} %fusion.33) | copy-start | bytes 294916
  176.5 4.4 %collective-permute-start.16 = (f32[3,8192]{1,0:T(4,128)S(1)}, f32[3,8192]{1,0:T(4,128)S(1)}, u32[]{:S(2)}, u32[]{:S(2)}) collective-permute-start(f32[3,8192]{1,0:T(4,128)S(1)} %bitcast.97), channel_id=1, source_target_pairs={{0,1},{1,2},{2,3},{3,0},{4,5},{5,6},{6,7},{7,4},{8,9},{9,10},{10,1... | collective-permute-start | bytes 294920 | tf_op jit(solution)/shard_map/ppermute | solution.py:109
  180.9 4.4 %collective-permute-start.17 = (f32[3,8192]{1,0:T(4,128)S(1)}, f32[3,8192]{1,0:T(4,128)S(1)}, u32[]{:S(2)}, u32[]{:S(2)}) collective-permute-start(f32[3,8192]{1,0:T(4,128)S(1)} %collective-permute-done.16), channel_id=1, source_target_pairs={{0,1},{1,2},{2,3},{3,0},{4,5},{5,6},{6,7},{7,4},{8,9},{9,10},{10,1... | collective-permute-start | bytes 294920 | tf_op jit(solution)/shard_map/ppermute | solution.py:109
  185.3 4.4 %collective-permute-start.18 = (f32[3,8192]{1,0:T(4,128)S(1)}, f32[3,8192]{1,0:T(4,128)S(1)}, u32[]{:S(2)}, u32[]{:S(2)}) collective-permute-start(f32[3,8192]{1,0:T(4,128)S(1)} %collective-permute-done.17), channel_id=1, source_target_pairs={{0,1},{1,2},{2,3},{3,0},{4,5},{5,6},{6,7},{7,4},{8,9},{9,10},{10,1... | collective-permute-start | bytes 294920 | tf_op jit(solution)/shard_map/ppermute | solution.py:109
Sparse Core Ops, SparseCore 0:
  105.8 69.5 all-reduce.3
